TPU v7x, 256 devices: a whole 4x4x8 slice. The times are simulated.
256 devices in a mesh: span: 8 (over z), xsec: 8 (over x, core), leaf: 4 (over y).
Axes of the slice: x: 4, y: 4, z: 8, core: 2. Of those that a mesh axis runs over, the one named last changes fastest.
Arguments:
- snapshots: float32 [3, 65536, 256], P(None, ('span', 'xsec', 'leaf')), may hold values from -1800 to 1800
- member_ends: int32 [2, 262144], P(None, ('span', 'xsec', 'leaf')), may hold values from 0 to 383, as said below
- member_dir: float32 [3, 262144], P(None, ('span', 'xsec', 'leaf')), may hold values from -3 to 3
- member_stiff: float32 [262144], P(('span', 'xsec', 'leaf')), may hold values from 0.25 to 24
Outputs:
- basis: float32 [3, 65536, 256], P(None, ('span', 'xsec', 'leaf'))
- forces: float32 [3, 65536, 256], P(None, ('span', 'xsec', 'leaf'))
- reduced: float32 [256, 256], replicated
- coef: float32 [256, 256], replicated
- column_energy: float32 [256], replicated
Inputs may be any that keep to these rules, and one draw needn't show every extreme that they name: member_ends[0] names a node of the member's own device block; member_ends[1] names such a node or, from 256 on, a node of the top level of the slab directly below in the same sector; both ends of a member lie on the same or neighbouring levels.
All inputs are finite; a program needn't handle non-finite values.
Results may differ from a plain program's by a relative error of at most 0.0008.
Values sent between devices are 32-bit elements; how exact they have to be, the bound alone decides.
A program may use at most 64 MiB of HBM per device.

v0:
```python
import functools
import math

import jax
import jax.numpy as jnp
from jax import lax
from jax.experimental import pallas as pl
from jax.experimental.pallas import tpu as pltpu
from jax.sharding import Mesh
from jax.sharding import PartitionSpec as P

SEC_NODES = 128
XSEC = ("xsec_0", "xsec_1")
SPAN_XSEC_LEAF = ("span", "xsec_0", "xsec_1", "leaf")
TILE = 8
LANES = 128
CHUNK = 256

highest = lax.Precision.HIGHEST
f32 = jnp.float32


def shifted(array, axis, by):
    length = lax.axis_size(axis)
    pairs = [(i, i + by) for i in range(length) if 0 <= i + by < length]
    return lax.ppermute(array, axis, pairs)


def cut_along(array, dim, length):
    shape = array.shape
    blocks = array.reshape(*shape[:dim], length, shape[dim] // length, *shape[dim + 1 :])
    return jnp.moveaxis(blocks, dim, 0)


def sent_and_summed(array, axis, dim):
    length = lax.axis_size(axis)
    blocks = lax.all_to_all(cut_along(array, dim, length), axis, 0, 0, tiled=True)
    return jnp.sum(blocks, axis=0)


def sum_in_two_steps(array, axes, dim):
    far, near = axes
    blocks = cut_along(array, dim, lax.axis_size(far))
    nearer = sent_and_summed(blocks, near, dim + 1)
    arrived = lax.all_to_all(nearer, far, split_axis=0, concat_axis=0, tiled=True)
    return arrived.sum(axis=0)


def from_everyone(array, axis):
    length = lax.axis_size(axis)
    return lax.all_to_all(
        jnp.broadcast_to(array[None], (length, *array.shape)), axis, 0, 0, tiled=True
    )


def whole_of(array, axes):
    far, near = axes
    blocks = from_everyone(from_everyone(array, far), near)
    return blocks.swapaxes(0, 1).reshape(-1, *array.shape[1:])


def sum_by_parts(lines, axes):
    return whole_of(sum_in_two_steps(lines, axes, 0), axes)


def dot_f32(a, b, over_a=1, over_b=0):
    return lax.dot_general(
        a, b, (((over_a,), (over_b,)), ((), ())), precision=highest, preferred_element_type=f32
    )


def dot_bf16(a, b):
    return jnp.dot(a, b, preferred_element_type=f32)


def in_three(x):
    high = x.astype(jnp.bfloat16)
    rest = x - high.astype(f32)
    middle = rest.astype(jnp.bfloat16)
    return high, middle, (rest - middle.astype(f32)).astype(jnp.bfloat16)


def over_lanes(column):
    return jnp.broadcast_to(column, (TILE, LANES))


def over_rows(row):
    return jnp.broadcast_to(row, (TILE, LANES))


def factor_block(block):
    count = LANES // TILE
    lane = lax.broadcasted_iota(jnp.int32, (TILE, LANES), 1)
    sub = lax.broadcasted_iota(jnp.int32, (TILE, LANES), 0)
    left = [block[TILE * i : TILE * i + TILE, :] for i in range(count)]
    right = [jnp.where(lane == sub + TILE * i, 1.0, 0.0).astype(f32) for i in range(count)]
    for k in range(count):
        own_left, own_right = left[k], right[k]
        at = TILE * k
        columns = [over_lanes(own_left[:, at + j : at + j + 1]) for j in range(TILE)]
        pivot_left, pivot_right, pivot_columns, inverse = [], [], [], []
        scale = jnp.zeros((TILE, LANES), f32)
        for j in range(TILE):
            pivot = over_rows(columns[j][j : j + 1, :])
            inverse.append(1.0 / pivot)
            pivot_left.append(over_rows(own_left[j : j + 1, :]))
            pivot_right.append(over_rows(own_right[j : j + 1, :]))
            pivot_columns.append([over_rows(columns[l][j : j + 1, :]) for l in range(TILE)])
            factor = jnp.where(sub > j, columns[j] * inverse[j], 0.0)
            for l in range(j + 1, TILE):
                columns[l] = columns[l] - factor * pivot_columns[j][l]
            own_left = own_left - factor * pivot_left[j]
            own_right = own_right - factor * pivot_right[j]
            scale = jnp.where(sub == j, lax.rsqrt(pivot), scale)
        for i in range(k + 1, count):
            columns = [over_lanes(left[i][:, at + j : at + j + 1]) for j in range(TILE)]
            row_left, row_right = left[i], right[i]
            for j in range(TILE):
                factor = columns[j] * inverse[j]
                for l in range(j + 1, TILE):
                    columns[l] = columns[l] - factor * pivot_columns[j][l]
                row_left = row_left - factor * pivot_left[j]
                row_right = row_right - factor * pivot_right[j]
            left[i], right[i] = row_left, row_right
        left[k] = jnp.where(lane >= sub + at, own_left * scale, 0.0)
        right[k] = own_right * scale
    return jnp.concatenate(left, 0), jnp.concatenate(right, 0)


def factor_into(gram_ref, upper_ref, inverse_ref):
    upper_a, lower_a = factor_block(gram_ref[:LANES, :LANES])
    across = dot_f32(lower_a, gram_ref[:LANES, LANES:])
    upper_b, lower_b = factor_block(gram_ref[LANES:, LANES:] - dot_f32(across, across, 0, 0))
    zero = jnp.zeros((LANES, LANES), f32)
    upper_ref[:LANES, :LANES] = upper_a
    upper_ref[:LANES, LANES:] = across
    upper_ref[LANES:, :LANES] = zero
    upper_ref[LANES:, LANES:] = upper_b
    inverse_a, inverse_b = lower_a.T, lower_b.T
    inverse_ref[:LANES, :LANES] = inverse_a
    inverse_ref[:LANES, LANES:] = -dot_f32(inverse_a, dot_f32(across, inverse_b))
    inverse_ref[LANES:, :LANES] = zero
    inverse_ref[LANES:, LANES:] = inverse_b


def members_kernel(field, below, ends, direction, stiff, elongation, forces, parts):
    components, own, width = field.shape
    nodes = own + below.shape[1]
    members = ends.shape[1]
    for c in range(components):
        for start, ref in ((0, field), (own, below)):
            for p, part in enumerate(in_three(ref[c])):
                parts[p, c, start : start + ref.shape[1], :] = part
    table = jnp.concatenate(
        [direction[...], stiff[...], ends[...].astype(f32), jnp.zeros((2, members), f32)], 0
    ).T
    forces[...] = jnp.zeros_like(forces)
    for start in range(0, members, CHUNK):
        rows = slice(start, start + CHUNK)
        of = [table[rows, i : i + 1] for i in range(6)]
        node = lax.broadcasted_iota(jnp.int32, (CHUNK, nodes), 1).astype(f32)
        pick = jnp.where(node == of[4], 1.0, 0.0) - jnp.where(node == of[5], 1.0, 0.0)
        pick = pick.astype(jnp.bfloat16)
        node = lax.broadcasted_iota(jnp.int32, (nodes, CHUNK), 0)
        spread = jnp.where(node == ends[0:1, rows], 1.0, 0.0)
        spread = spread - jnp.where(node == ends[1:2, rows], 1.0, 0.0)
        spread = spread.astype(jnp.bfloat16)
        stretch = jnp.zeros((CHUNK, width), f32)
        for c in range(components):
            difference = dot_bf16(pick, parts[2, c])
            difference = difference + dot_bf16(pick, parts[1, c])
            difference = difference + dot_bf16(pick, parts[0, c])
            stretch = stretch + of[c] * difference
        elongation[rows, :] = stretch
        pull = stretch * of[3]
        for c in range(components):
            high, middle, low = in_three(of[c] * pull)
            push = dot_bf16(spread, low) + dot_bf16(spread, middle) + dot_bf16(spread, high)
            forces[c] = forces[c] + push


def member_forces(field, below, ends, direction, stiff):
    components, own, width = field.shape
    nodes, members = own + below.shape[1], ends.shape[1]
    return pl.pallas_call(
        members_kernel,
        out_shape=(
            jax.ShapeDtypeStruct((members, width), f32),
            jax.ShapeDtypeStruct((components, nodes, width), f32),
        ),
        scratch_shapes=[pltpu.VMEM((3, components, nodes, width), jnp.bfloat16)],
        compiler_params=pltpu.CompilerParams(vmem_limit_bytes=60 << 20),
        cost_estimate=pl.CostEstimate(
            flops=12 * components * nodes * members * width, bytes_accessed=4 << 20, transcendentals=0
        ),
        name="member_forces",
    )(field, below, ends, direction, stiff.reshape(1, -1))


def first_kernel(gram, field, elongation, stiff, upper, inverse, first, sums):
    factor_into(gram, upper, inverse)
    transform = inverse[...]
    width = transform.shape[0]
    first[...] = dot_f32(field[...], transform)
    sums[:width, :] = dot_f32(first[...], first[...], 0, 0)
    stretch = dot_f32(elongation[...], transform)
    sums[width:, :] = dot_f32(stretch, stretch * stiff[...].T[:, :1], 0, 0)


def first_pass(gram, flattened, elongation, stiff):
    rows, width = flattened.shape
    square = jax.ShapeDtypeStruct((width, width), f32)
    stiff = jnp.broadcast_to(stiff.reshape(1, -1), (TILE, stiff.shape[0]))
    return pl.pallas_call(
        first_kernel,
        out_shape=(
            square,
            square,
            jax.ShapeDtypeStruct((rows, width), f32),
            jax.ShapeDtypeStruct((2 * width, width), f32),
        ),
        compiler_params=pltpu.CompilerParams(vmem_limit_bytes=60 << 20),
        name="first_pass",
    )(gram, flattened, elongation, stiff)


def second_kernel(
    total_rows, own, sums, upper_first, inverse_first, first, raw, returned, basis, forces, reduced,
    coef, upper, inverse,
):
    width = inverse.shape[0]
    root = math.sqrt(total_rows)
    factor_into(sums.at[:width, :], upper, inverse)
    transform = inverse[...]
    basis[...] = dot_f32(first[...], transform) * root
    both = dot_f32(inverse_first[...], transform) * root
    for c in range(raw.shape[0]):
        low = own - returned.shape[1]
        forces[c, :low, :] = dot_f32(raw[c, :low, :], both)
        forces[c, low:, :] = dot_f32(raw[c, low:own, :] + returned[c], both)
    reduced[...] = dot_f32(transform, dot_f32(sums[width:, :], transform), 0, 0)
    coef[...] = dot_f32(upper[...], upper_first[...]) * (1.0 / root)


def second_pass(sums, upper, inverse, first, raw, returned, total_rows):
    components, _, width = raw.shape
    own = first.shape[0] // components
    square = jax.ShapeDtypeStruct((width, width), f32)
    return pl.pallas_call(
        functools.partial(second_kernel, total_rows, own),
        out_shape=(
            jax.ShapeDtypeStruct(first.shape, f32),
            jax.ShapeDtypeStruct((components, own, width), f32),
            square,
            square,
        ),
        scratch_shapes=[pltpu.VMEM((width, width), f32)] * 2,
        compiler_params=pltpu.CompilerParams(vmem_limit_bytes=60 << 20),
        name="second_pass",
    )(sums, upper, inverse, first, raw, returned)


def local(snapshots, member_ends, member_dir, member_stiff):
    components, node_count, width = snapshots.shape
    flattened = snapshots.reshape(components * node_count, width)
    devices_all = lax.axis_size("span") * lax.axis_size(XSEC) * lax.axis_size("leaf")
    total_rows = components * node_count * devices_all
    axes = (("span", "xsec_0"), ("xsec_1", "leaf"))
    below = shifted(snapshots[:, node_count - SEC_NODES :, :], "span", 1)
    gram = sum_by_parts(dot_f32(flattened, flattened, 0, 0), axes)
    column_energy = jnp.log(jnp.diagonal(gram) / total_rows)
    elongation, raw = member_forces(snapshots, below, member_ends, member_dir, member_stiff)
    returned = shifted(raw[:, node_count:, :], "span", -1)
    upper, inverse, first, sums = first_pass(gram, flattened, elongation, member_stiff)
    sums = sum_by_parts(sums, axes)
    basis, forces, reduced, coef = second_pass(
        sums, upper, inverse, first, raw, returned, total_rows
    )
    return (basis.reshape(snapshots.shape), forces, reduced, coef, column_energy)


def solution(mesh):
    torus = Mesh(
        mesh.devices.reshape(mesh.shape["span"], 4, 2, mesh.shape["leaf"]),
        ("span", "xsec_0", "xsec_1", "leaf"),
    )
    return jax.shard_map(
        local,
        mesh=torus,
        in_specs=(
            P(None, SPAN_XSEC_LEAF, None),
            P(None, SPAN_XSEC_LEAF),
            P(None, SPAN_XSEC_LEAF),
            P(SPAN_XSEC_LEAF),
        ),
        out_specs=(P(None, SPAN_XSEC_LEAF, None), P(None, SPAN_XSEC_LEAF, None), P(), P(), P()),
        check_vma=False,
    )
```

profile of v0, /device:TPU:1, one launch (start us, length us, event | category | flops | bytes accessed | tf_op | source)
XLA Modules:
  0.0 158.6 jit_solution(4844389865446827782)
XLA Ops:
  0.6 1.1 slice.6
  1.7 4.4 %collective-permute-start = (f32[3,128,256]{2,1,0:T(8,128)S(1)}, f32[3,128,256]{2,1,0:T(8,128)S(1)}, u32[]{:S(2)}, u32[]{:S(2)}) collective-permute-start(f32[3,128,256]{2,1,0:T(8,128)S(1)} %slice.6), channel_id=1, source_target_pairs={{0,32},{32,64},{64,96},{96,128},{128,160},{160,192},{192,224},{1,3... | collective-permute-start | bytes 1179656 | tf_op jit(solution)/shard_map/ppermute | solution.py:26
  6.4 0.8 convolution_bitcast_fusion
  7.3 11.7 %all_to_all.40 = f32[8,32,1,256]{3,1,2,0:T(8,128)S(1)} all-to-all(f32[8,32,1,256]{3,1,2,0:T(8,128)S(1)} %copy.22), channel_id=1, replica_groups=mesh['span'=8,'xsec_0'=4,'xsec_1'=2,'leaf'=4] {'xsec_1','leaf'}, dimensions={0} | all-to-all | bytes 524288 | tf_op jit(solution)/shard_map/all_to_all | solution.py:37
  19.1 18.6 %all_to_all.41 = f32[32,1,256]{2,1,0:T(1,128)S(1)} all-to-all(f32[32,1,256]{2,1,0:T(1,128)S(1)} %reduce_sum.39), channel_id=1, replica_groups=mesh['span'=8,'xsec_0'=4,'xsec_1'=2,'leaf'=4] {'span','xsec_0'}, dimensions={0} | all-to-all | bytes 65536 | tf_op jit(solution)/shard_map/all_to_all | solution.py:45
  37.8 11.6 %all_to_all.42 = f32[32,1,256]{2,1,0:T(1,128)S(1)} all-to-all(f32[32,1,256]{2,1,0:T(1,128)S(1)} %broadcast_in_dim.16), channel_id=1, replica_groups=mesh['span'=8,'xsec_0'=4,'xsec_1'=2,'leaf'=4] {'span','xsec_0'}, dimensions={0} | all-to-all | bytes 65536 | tf_op jit(solution)/shard_map/all_to_all | solution.py:51
  50.2 6.2 %all-to-all-start.3 = ((f32[8,32,1,256]{3,1,2,0:T(8,128)}), f32[8,32,1,256]{3,1,2,0:T(8,128)S(1)}, u32[]{:S(2)}, u32[]{:S(2)}) async-start(f32[8,32,1,256]{3,1,2,0:T(8,128)} %broadcast_in_dim.18), calls=%async_computation.3 | async-start | bytes 524288 | tf_op jit(solution)/shard_map/all_to_all | solution.py:51
  56.4 0.7 copy-done.4
  57.1 8.7 %member_forces.1 = (f32[1024,256]{1,0:T(8,128)}, f32[3,384,256]{2,1,0:T(8,128)}) custom-call(f32[3,256,256]{2,1,0:T(8,128)} %field.1, f32[3,128,256]{2,1,0:T(8,128)} %copy-done.4, s32[2,1024]{1,0:T(2,128)} %ends.1, f32[3,1024]{1,0:T(4,128)} %direction.1, f32[1,1024]{1,0:T(1,128)} %bitcast.37), custom_call_target="tpu_custom_call" | custom-call | flops 3623878656 | bytes 4194304 | tf_op jit(solution)/shard_map/member_forces/pallas_call | solution.py:185
  65.8 0.9 copy.33
  67.3 16.5 %first_pass.1 = (f32[256,256]{1,0:T(8,128)}, f32[256,256]{1,0:T(8,128)}, f32[768,256]{1,0:T(8,128)}, f32[512,256]{1,0:T(8,128)}) custom-call(f32[256,256]{1,0:T(8,128)} %bitcast.31, f32[768,256]{1,0:T(8,128)} %bitcast.28, f32[1024,256]{1,0:T(8,128)} %get-tuple-element.15.elongation, f32[8,1024]{1,0:T(8,128)} %broadcast_in_dim.19.stiff), custom_call_target="tpu_custom_call" | custom-call | tf_op jit(solution)/shard_map/first_pass/pallas_call | solution.py:214
  83.8 1.3 reshape_reshape.4
  85.3 13.9 %all_to_all.43 = f32[8,32,2,256]{3,2,1,0:T(2,128)S(1)} all-to-all(f32[8,32,2,256]{3,2,1,0:T(2,128)S(1)} %bitcast.34), channel_id=1, replica_groups=mesh['span'=8,'xsec_0'=4,'xsec_1'=2,'leaf'=4] {'xsec_1','leaf'}, dimensions={0} | all-to-all | bytes 1048576 | tf_op jit(solution)/shard_map/all_to_all | solution.py:37
  99.4 12.0 %all_to_all.44 = f32[32,2,256]{2,1,0:T(2,128)S(1)} all-to-all(f32[32,2,256]{2,1,0:T(2,128)S(1)} %reduce_sum.41), channel_id=1, replica_groups=mesh['span'=8,'xsec_0'=4,'xsec_1'=2,'leaf'=4] {'span','xsec_0'}, dimensions={0} | all-to-all | bytes 131072 | tf_op jit(solution)/shard_map/all_to_all | solution.py:45
  111.5 11.8 %all_to_all.45 = f32[32,2,256]{2,1,0:T(2,128)S(1)} all-to-all(f32[32,2,256]{2,1,0:T(2,128)S(1)} %broadcast_in_dim.20), channel_id=1, replica_groups=mesh['span'=8,'xsec_0'=4,'xsec_1'=2,'leaf'=4] {'span','xsec_0'}, dimensions={0} | all-to-all | bytes 131072 | tf_op jit(solution)/shard_map/all_to_all | solution.py:51
  123.3 0.9 broadcast_in_dim.21
  124.2 6.0 %all-to-all-start.7 = ((f32[8,32,2,256]{3,2,1,0:T(2,128)}), f32[8,32,2,256]{3,2,1,0:T(2,128)S(1)}, u32[]{:S(2)}, u32[]{:S(2)}) async-start(f32[8,32,2,256]{3,2,1,0:T(2,128)} %broadcast_in_dim.21), calls=%async_computation.7 | async-start | bytes 1048576 | tf_op jit(solution)/shard_map/all_to_all | solution.py:51
  130.2 1.0 slice.7
  131.2 1.3 collective-permute-start.1
  132.6 2.3 %gather_fusion = f32[256]{0:T(256)S(1)} fusion(f32[256,256]{1,0:T(8,128)S(1)} %bitcast.32, s32[256]{0:T(256)S(1)} %bitcast.27), kind=kCustom, calls=%fused_computation | custom fusion | bytes 4096 | tf_op jit(solution)/shard_map/jit(diagonal)/cond/branch_0_fun/gather | solution.py:271
  135.5 4.1 %all-to-all-done.7 = f32[8,32,2,256]{3,2,1,0:T(2,128)S(1)} async-done(((f32[8,32,2,256]{3,2,1,0:T(2,128)}), f32[8,32,2,256]{3,2,1,0:T(2,128)S(1)}, u32[]{:S(2)}, u32[]{:S(2)}) %all-to-all-start.7) | async-done | bytes 524320 | tf_op jit(solution)/shard_map/all_to_all | solution.py:51
  139.9 1.2 reshape.46.sums
  141.1 2.7 %collective-permute-done.1.returned = f32[3,128,256]{2,1,0:T(8,128)S(1)} collective-permute-done((f32[3,128,256]{2,1,0:T(8,128)S(1)}, f32[3,128,256]{2,1,0:T(8,128)S(1)}, u32[]{:S(2)}, u32[]{:S(2)}) %collective-permute-start.1) | collective-permute-done | bytes 393248 | tf_op jit(solution)/shard_map/ppermute | solution.py:26
  144.5 14.2 %second_pass.1 = (f32[768,256]{1,0:T(8,128)}, f32[3,256,256]{2,1,0:T(8,128)}, f32[256,256]{1,0:T(8,128)}, f32[256,256]{1,0:T(8,128)}) custom-call(f32[512,256]{1,0:T(8,128)} %reshape.46.sums, f32[256,256]{1,0:T(8,128)} %get-tuple-element.17.upper_first, f32[256,256]{1,0:T(8,128)} %get-tuple-element.18.inverse_first, f32[768,256]{1,0:T(8,128)} %get-tuple-element.19.first, ...), custom_call_target="tpu_custom_call" | custom-call | tf_op jit(solution)/shard_map/second_pass/pallas_call | solution.py:249
  (27 shorter events, 3.9 us)
Async XLA Ops:
  0.6 5.5 %copy-start = (f32[3,256,256]{2,1,0:T(8,128)S(1)}, f32[3,256,256]{2,1,0:T(8,128)}, u32[]{:S(2)}) copy-start(f32[3,256,256]{2,1,0:T(8,128)} %field.1) | copy-start | bytes 2359300
  1.7 54.6 %collective-permute-start = (f32[3,128,256]{2,1,0:T(8,128)S(1)}, f32[3,128,256]{2,1,0:T(8,128)S(1)}, u32[]{:S(2)}, u32[]{:S(2)}) collective-permute-start(f32[3,128,256]{2,1,0:T(8,128)S(1)} %slice.6), channel_id=1, source_target_pairs={{0,32},{32,64},{64,96},{96,128},{128,160},{160,192},{192,224},{1,3... | collective-permute-start | bytes 1179656 | tf_op jit(solution)/shard_map/ppermute | solution.py:26
  50.2 15.7 %all-to-all-start.3 = ((f32[8,32,1,256]{3,1,2,0:T(8,128)}), f32[8,32,1,256]{3,1,2,0:T(8,128)S(1)}, u32[]{:S(2)}, u32[]{:S(2)}) async-start(f32[8,32,1,256]{3,1,2,0:T(8,128)} %broadcast_in_dim.18), calls=%async_computation.3 | async-start | bytes 524288 | tf_op jit(solution)/shard_map/all_to_all | solution.py:51
  56.4 0.7 copy-start.4
  57.1 9.6 %copy-start.3 = (f32[1024]{0:T(1024)S(1)}, f32[1024]{0:T(1024)}, u32[]{:S(2)}) copy-start(f32[1024]{0:T(1024)} %param.7) | copy-start | bytes 12292
  123.3 9.3 %copy-start.1 = (f32[32,8,1,256]{3,1,0,2:T(8,128)S(1)}, f32[32,8,1,256]{3,1,0,2:T(8,128)}, u32[]{:S(2)}) copy-start(f32[32,8,1,256]{3,1,0,2:T(8,128)} %copy.33) | copy-start | bytes 786436
  124.2 15.3 %all-to-all-start.7 = ((f32[8,32,2,256]{3,2,1,0:T(2,128)}), f32[8,32,2,256]{3,2,1,0:T(2,128)S(1)}, u32[]{:S(2)}, u32[]{:S(2)}) async-start(f32[8,32,2,256]{3,2,1,0:T(2,128)} %broadcast_in_dim.21), calls=%async_computation.7 | async-start | bytes 1048576 | tf_op jit(solution)/shard_map/all_to_all | solution.py:51
  131.2 12.5 %collective-permute-start.1 = (f32[3,128,256]{2,1,0:T(8,128)S(1)}, f32[3,128,256]{2,1,0:T(8,128)S(1)}, u32[]{:S(2)}, u32[]{:S(2)}) collective-permute-start(f32[3,128,256]{2,1,0:T(8,128)S(1)} %slice.7), channel_id=1, source_target_pairs={{32,0},{64,32},{96,64},{128,96},{160,128},{192,160},{224,192},{33,... | collective-permute-start | bytes 1179656 | tf_op jit(solution)/shard_map/ppermute | solution.py:26
  143.7 0.7 copy-start.2
where the time goes:
time: 159 us
  blocking collectives  79.7 us (50%)
  Pallas kernels  39.4 us (25%)
  starting transfers between devices  17.9 us (11%)
  local copies, waits for them, and re-layouts  12.5 us (8%)
  waiting for transfers between devices  6.74 us (4%)
    all_to_all x2, blocking collectives, sum_in_two_steps(): lax.all_to_all(nearer, far, split_axis=0, concat_axis=0, tiled=True)  30.6 us
    all_to_all x2, blocking collectives, sent_and_summed(): lax.all_to_all(cut_along(array, dim, length), axis, 0, 0, tiled=True)  25.7 us
    all_to_all x2, blocking collectives, from_everyone(): lax.all_to_all(jnp.broadcast_to(array[None], (length, *array.shape)), axi...  23.4 us
    pallas_call x1, Pallas kernels, first_pass(): pl.pallas_call(first_kernel, out_shape=(square, square, jax.ShapeDtypeStr...  16.5 us
    pallas_call x1, Pallas kernels, second_pass(): pl.pallas_call(functools.partial(second_kernel, total_rows, own), out_sha...  14.2 us
    all_to_all x2, starting transfers between devices, from_everyone(): lax.all_to_all(jnp.broadcast_to(array[None], (length, *array.shape)), axi...  12.2 us
    pallas_call x1, Pallas kernels, member_forces(): pl.pallas_call(members_kernel, out_shape=(jax.ShapeDtypeStruct((members,...  8.72 us
    ppermute x2, starting transfers between devices, shifted(): return lax.ppermute(array, axis, pairs)  5.68 us
  transfers between devices with their start and end apart: 4, of which 2 were waited for; matrix products, arithmetic and copies ran while one was open for 5% of the time, Pallas kernels for 5%

commit v1 on v0

--- a/solution.py
+++ b/solution.py
@@ -6,12 +6,10 @@
 from jax import lax
 from jax.experimental import pallas as pl
 from jax.experimental.pallas import tpu as pltpu
-from jax.sharding import Mesh
 from jax.sharding import PartitionSpec as P
 
 SEC_NODES = 128
-XSEC = ("xsec_0", "xsec_1")
-SPAN_XSEC_LEAF = ("span", "xsec_0", "xsec_1", "leaf")
+SPAN_XSEC_LEAF = ("span", "xsec", "leaf")
 TILE = 8
 LANES = 128
 CHUNK = 256
@@ -26,41 +24,85 @@
     return lax.ppermute(array, axis, pairs)
 
 
-def cut_along(array, dim, length):
-    shape = array.shape
-    blocks = array.reshape(*shape[:dim], length, shape[dim] // length, *shape[dim + 1 :])
-    return jnp.moveaxis(blocks, dim, 0)
-
-
-def sent_and_summed(array, axis, dim):
-    length = lax.axis_size(axis)
-    blocks = lax.all_to_all(cut_along(array, dim, length), axis, 0, 0, tiled=True)
-    return jnp.sum(blocks, axis=0)
-
-
-def sum_in_two_steps(array, axes, dim):
-    far, near = axes
-    blocks = cut_along(array, dim, lax.axis_size(far))
-    nearer = sent_and_summed(blocks, near, dim + 1)
-    arrived = lax.all_to_all(nearer, far, split_axis=0, concat_axis=0, tiled=True)
-    return arrived.sum(axis=0)
-
-
-def from_everyone(array, axis):
-    length = lax.axis_size(axis)
-    return lax.all_to_all(
-        jnp.broadcast_to(array[None], (length, *array.shape)), axis, 0, 0, tiled=True
-    )
-
-
-def whole_of(array, axes):
-    far, near = axes
-    blocks = from_everyone(from_everyone(array, far), near)
-    return blocks.swapaxes(0, 1).reshape(-1, *array.shape[1:])
-
-
-def sum_by_parts(lines, axes):
-    return whole_of(sum_in_two_steps(lines, axes, 0), axes)
+def all_sum_kernel(part, total, arrived, planes, gathered, sent, got):
+    near, far = part.shape[0], planes.shape[0]
+    leaves = lax.axis_size("leaf")
+    chips = near // (2 * leaves)
+    span, xsec, leaf = (lax.axis_index(name) for name in ("span", "xsec", "leaf"))
+    chip, core = xsec // 2, xsec % 2
+    own = xsec * leaves + leaf
+
+    def place(step):
+        there = (chip + (step // 2) % chips) % chips
+        return there * 2 + (core + step % 2) % 2, (leaf + step // (2 * chips)) % leaves
+
+    def in_slab(step):
+        other, side = place(step)
+        return {"xsec": other, "leaf": side}
+
+    def over_slabs(step):
+        return {"span": (span + step) % far}
+
+    def scatter(step):
+        other, side = place(step)
+        return pltpu.make_async_remote_copy(
+            part.at[other * leaves + side], arrived.at[step], sent.at[0, step], got.at[0, step],
+            in_slab(step),
+        )
+
+    def exchange(step):
+        return pltpu.make_async_remote_copy(
+            planes.at[span], planes.at[span], sent.at[1, step], got.at[1, step], over_slabs(step)
+        )
+
+    def gather(step):
+        return pltpu.make_async_remote_copy(
+            gathered.at[own], gathered.at[own], sent.at[2, step], got.at[2, step], in_slab(step)
+        )
+
+    def each(count, act):
+        lax.fori_loop(1, count, lambda step, _: (act(step), 0)[1], 0)
+
+    barrier = pltpu.get_barrier_semaphore()
+    each(near, lambda step: pl.semaphore_signal(barrier, inc=1, device_id=in_slab(step)))
+    each(far, lambda step: pl.semaphore_signal(barrier, inc=1, device_id=over_slabs(step)))
+    pl.semaphore_wait(barrier, near + far - 2)
+    each(near, lambda step: scatter(step).start())
+    each(near, lambda step: scatter(step).wait_recv())
+    block = part[own]
+    for step in range(1, near):
+        block = block + arrived[step]
+    planes[span] = block
+    each(far, lambda step: exchange(step).start())
+    each(far, lambda step: exchange(step).wait_recv())
+    block = planes[0]
+    for other in range(1, far):
+        block = block + planes[other]
+    gathered[own] = block
+    each(near, lambda step: gather(step).start())
+    each(near, lambda step: gather(step).wait_recv())
+    total[...] = gathered[...]
+    each(near, lambda step: scatter(step).wait_send())
+    each(far, lambda step: exchange(step).wait_send())
+    each(near, lambda step: gather(step).wait_send())
+
+
+def all_sum(blocks, key):
+    near, lines, lanes = blocks.shape
+    far = lax.axis_size("span")
+    return pl.pallas_call(
+        all_sum_kernel,
+        out_shape=jax.ShapeDtypeStruct(blocks.shape, f32),
+        scratch_shapes=[
+            pltpu.VMEM(blocks.shape, f32),
+            pltpu.VMEM((far, lines, lanes), f32),
+            pltpu.VMEM(blocks.shape, f32),
+            pltpu.SemaphoreType.DMA((3, near)),
+            pltpu.SemaphoreType.DMA((3, near)),
+        ],
+        compiler_params=pltpu.CompilerParams(collective_id=key, has_side_effects=True),
+        name="all_sum",
+    )(blocks)
 
 
 def dot_f32(a, b, over_a=1, over_b=0):
@@ -263,16 +305,17 @@
 def local(snapshots, member_ends, member_dir, member_stiff):
     components, node_count, width = snapshots.shape
     flattened = snapshots.reshape(components * node_count, width)
-    devices_all = lax.axis_size("span") * lax.axis_size(XSEC) * lax.axis_size("leaf")
+    devices_all = lax.axis_size("span") * lax.axis_size("xsec") * lax.axis_size("leaf")
     total_rows = components * node_count * devices_all
-    axes = (("span", "xsec_0"), ("xsec_1", "leaf"))
     below = shifted(snapshots[:, node_count - SEC_NODES :, :], "span", 1)
-    gram = sum_by_parts(dot_f32(flattened, flattened, 0, 0), axes)
+    near = lax.axis_size("xsec") * lax.axis_size("leaf")
+    gram = dot_f32(flattened, flattened, 0, 0)
+    gram = all_sum(gram.reshape(near, -1, LANES), 0).reshape(gram.shape)
     column_energy = jnp.log(jnp.diagonal(gram) / total_rows)
     elongation, raw = member_forces(snapshots, below, member_ends, member_dir, member_stiff)
     returned = shifted(raw[:, node_count:, :], "span", -1)
     upper, inverse, first, sums = first_pass(gram, flattened, elongation, member_stiff)
-    sums = sum_by_parts(sums, axes)
+    sums = all_sum(sums.reshape(near, -1, LANES), 1).reshape(sums.shape)
     basis, forces, reduced, coef = second_pass(
         sums, upper, inverse, first, raw, returned, total_rows
     )
@@ -280,13 +323,9 @@
 
 
 def solution(mesh):
-    torus = Mesh(
-        mesh.devices.reshape(mesh.shape["span"], 4, 2, mesh.shape["leaf"]),
-        ("span", "xsec_0", "xsec_1", "leaf"),
-    )
     return jax.shard_map(
         local,
-        mesh=torus,
+        mesh=mesh,
         in_specs=(
             P(None, SPAN_XSEC_LEAF, None),
             P(None, SPAN_XSEC_LEAF),

time: 159 us -> 133 us (0.84)
  blocking collectives: 79.7 us -> 0 us
  Pallas kernels: 39.4 us -> 104 us
  starting transfers between devices: 17.9 us -> 5.68 us
    all_to_all x6 -> x0, blocking collectives: 79.7 us -> none  [the longest x2 30.6 us: sum_in_two_steps(): lax.all_to_all(nearer, far, split_axis=0, concat_axis=0, tiled=True)]
    pallas_call x0 -> x2, Pallas kernels: none -> 64.8 us  [all_sum(): pl.pallas_call(all_sum_kernel, out_shape=jax.ShapeDtypeStruct(blocks.shap...]
    all_to_all x2 -> x0, starting transfers between devices: 12.2 us -> none  [from_everyone(): lax.all_to_all(jnp.broadcast_to(array[None], (length, *array.shape)), axi...]
    ppermute x2, waiting for transfers between devices: 2.65 us -> 7.76 us  [shifted(): return lax.ppermute(array, axis, pairs)]
    reshape x1 -> x4, local copies, waits for them, and re-layouts: 1.2 us -> 5.63 us  [the longest x2 3.88 us: local(): sums = all_sum(sums.reshape(near, -1, LANES), 1).reshape(sums.shape)]
    all_to_all x2 -> x0, waiting for transfers between devices: 4.09 us -> none  [from_everyone(): lax.all_to_all(jnp.broadcast_to(array[None], (length, *array.shape)), axi...]
    broadcast_in_dim x4 -> x0, local copies, waits for them, and re-layouts: 1.7 us -> none  [from_everyone(): jnp.broadcast_to(array[None], (length, *array.shape))]
  transfers between devices with their start and end apart: 4 -> 2, of which waited for: 2 -> 1; matrix products, arithmetic and copies ran while one was open for 5% -> 8% of each run, Pallas kernels for 5% -> 61%
where the time goes in v1:
time: 133 us; the launch traced here: 132 us
  Pallas kernels  104 us (78%)
  local copies, waits for them, and re-layouts  12.4 us (9%)
  waiting for transfers between devices  7.76 us (6%)
  starting transfers between devices  5.68 us (4%)
  matrix products  1.43 us (1%)
    pallas_call x2, Pallas kernels, all_sum(): pl.pallas_call(all_sum_kernel, out_shape=jax.ShapeDtypeStruct(blocks.shap...  64.8 us
    pallas_call x1, Pallas kernels, first_pass(): pl.pallas_call(first_kernel, out_shape=(square, square, jax.ShapeDtypeStr...  16.2 us
    pallas_call x1, Pallas kernels, second_pass(): pl.pallas_call(functools.partial(second_kernel, total_rows, own), out_sha...  14.2 us
    pallas_call x1, Pallas kernels, member_forces(): pl.pallas_call(members_kernel, out_shape=(jax.ShapeDtypeStruct((members,...  8.72 us
    ppermute x2, waiting for transfers between devices, shifted(): return lax.ppermute(array, axis, pairs)  7.76 us
    ppermute x2, starting transfers between devices, shifted(): return lax.ppermute(array, axis, pairs)  5.68 us
    reshape x2, local copies, waits for them, and re-layouts, local(): sums = all_sum(sums.reshape(near, -1, LANES), 1).reshape(sums.shape)  3.88 us
  transfers between devices with their start and end apart: 2, of which 1 were waited for; matrix products, arithmetic and copies ran while one was open for 8% of the time, Pallas kernels for 61%

profile of v1, /device:TPU:1, one launch (start us, length us, event | category | flops | bytes accessed | tf_op | source)
XLA Modules:
  0.0 132.5 jit_solution(4378257136737846793)
XLA Ops:
  0.6 1.0 slice.6
  1.7 4.4 %collective-permute-start = (f32[3,128,256]{2,1,0:T(8,128)S(1)}, f32[3,128,256]{2,1,0:T(8,128)S(1)}, u32[]{:S(2)}, u32[]{:S(2)}) collective-permute-start(f32[3,128,256]{2,1,0:T(8,128)S(1)} %slice.6), channel_id=1, source_target_pairs={{0,32},{32,64},{64,96},{96,128},{128,160},{160,192},{192,224},{1,3... | collective-permute-start | bytes 1179656 | tf_op jit(solution)/shard_map/ppermute | solution.py:24
  6.1 7.8 %collective-permute-done.below = f32[3,128,256]{2,1,0:T(8,128)S(1)} collective-permute-done((f32[3,128,256]{2,1,0:T(8,128)S(1)}, f32[3,128,256]{2,1,0:T(8,128)S(1)}, u32[]{:S(2)}, u32[]{:S(2)}) %collective-permute-start) | collective-permute-done | bytes 393248 | tf_op jit(solution)/shard_map/ppermute | solution.py:24
  13.8 0.7 copy-done.4
  14.6 8.7 %member_forces.1 = (f32[1024,256]{1,0:T(8,128)}, f32[3,384,256]{2,1,0:T(8,128)}) custom-call(f32[3,256,256]{2,1,0:T(8,128)} %field.1, f32[3,128,256]{2,1,0:T(8,128)} %copy-done.4, s32[2,1024]{1,0:T(2,128)} %ends.1, f32[3,1024]{1,0:T(4,128)} %direction.1, f32[1,1024]{1,0:T(1,128)} %bitcast.10), custom_call_target="tpu_custom_call" | custom-call | flops 3623878656 | bytes 4194304 | tf_op jit(solution)/shard_map/member_forces/pallas_call | solution.py:227
  23.3 1.1 slice.7
  24.4 1.3 collective-permute-start.1
  25.7 0.0 copy-done
  25.7 1.4 %convolution_bitcast_fusion = f32[256,256]{1,0:T(8,128)S(1)} fusion(f32[3,256,256]{2,1,0:T(8,128)S(1)} %copy-done), kind=kOutput, calls=%fused_computation.1 | convolution fusion | flops 603979776 | bytes 1048576 | tf_op jit(solution)/shard_map/dot_general | solution.py:109
  27.1 0.7 reshape.33.part
  27.8 35.2 %all_sum.2 = f32[32,16,128]{2,1,0:T(8,128)} custom-call(f32[32,16,128]{2,1,0:T(8,128)} %reshape.33.part), custom_call_target="tpu_custom_call" | custom-call | tf_op jit(solution)/shard_map/all_sum/pallas_call | solution.py:93
  63.0 1.0 reshape.34.gram
  64.1 0.0 copy-start.1
  64.1 2.5 %gather_fusion = f32[256]{0:T(256)S(1)} fusion(f32[256,256]{1,0:T(8,128)S(1)} %reshape.34.gram, s32[256]{0:T(256)S(1)} %bitcast.8), kind=kCustom, calls=%fused_computation | custom fusion | bytes 4096 | tf_op jit(solution)/shard_map/jit(diagonal)/cond/branch_0_fun/gather | solution.py:314
  66.6 0.6 multiply_log_fusion
  67.2 0.6 broadcast_in_dim.6.stiff
  67.8 0.0 copy-done.1
  67.8 16.2 %first_pass.1 = (f32[256,256]{1,0:T(8,128)}, f32[256,256]{1,0:T(8,128)}, f32[768,256]{1,0:T(8,128)}, f32[512,256]{1,0:T(8,128)}) custom-call(f32[256,256]{1,0:T(8,128)} %copy-done.1, f32[768,256]{1,0:T(8,128)} %bitcast.9, f32[1024,256]{1,0:T(8,128)} %get-tuple-element.15.elongation, f32[8,1024]{1,0:T(8,128)} %broadcast_in_dim.6.stiff), custom_call_target="tpu_custom_call" | custom-call | tf_op jit(solution)/shard_map/first_pass/pallas_call | solution.py:256
  84.1 1.9 %reshape.37.part = f32[32,32,128]{2,1,0:T(8,128)} reshape(f32[512,256]{1,0:T(8,128)} %get-tuple-element.16) | data formatting | bytes 1048576 | tf_op jit(solution)/shard_map/reshape | solution.py:318
  85.9 29.6 %all_sum.3 = f32[32,32,128]{2,1,0:T(8,128)} custom-call(f32[32,32,128]{2,1,0:T(8,128)} %reshape.37.part), custom_call_target="tpu_custom_call" | custom-call | tf_op jit(solution)/shard_map/all_sum/pallas_call | solution.py:93
  115.6 2.0 %reshape.38.sums = f32[512,256]{1,0:T(8,128)} reshape(f32[32,32,128]{2,1,0:T(8,128)} %all_sum.3) | data formatting | bytes 1048576 | tf_op jit(solution)/shard_map/reshape | solution.py:318
  117.6 0.0 collective-permute-done.1.returned
  117.6 0.7 copy-done.2
  118.3 14.2 %second_pass.1 = (f32[768,256]{1,0:T(8,128)}, f32[3,256,256]{2,1,0:T(8,128)}, f32[256,256]{1,0:T(8,128)}, f32[256,256]{1,0:T(8,128)}) custom-call(f32[512,256]{1,0:T(8,128)} %reshape.38.sums, f32[256,256]{1,0:T(8,128)} %get-tuple-element.17.upper_first, f32[256,256]{1,0:T(8,128)} %get-tuple-element.18.inverse_first, f32[768,256]{1,0:T(8,128)} %get-tuple-element.19.first, ...), custom_call_target="tpu_custom_call" | custom-call | tf_op jit(solution)/shard_map/second_pass/pallas_call | solution.py:291
  (6 shorter events, 0.0 us)
Async XLA Ops:
  1.7 12.1 %collective-permute-start = (f32[3,128,256]{2,1,0:T(8,128)S(1)}, f32[3,128,256]{2,1,0:T(8,128)S(1)}, u32[]{:S(2)}, u32[]{:S(2)}) collective-permute-start(f32[3,128,256]{2,1,0:T(8,128)S(1)} %slice.6), channel_id=1, source_target_pairs={{0,32},{32,64},{64,96},{96,128},{128,160},{160,192},{192,224},{1,3... | collective-permute-start | bytes 1179656 | tf_op jit(solution)/shard_map/ppermute | solution.py:24
  13.8 0.7 copy-start.4
  23.3 2.4 %copy-start = (f32[3,256,256]{2,1,0:T(8,128)S(1)}, f32[3,256,256]{2,1,0:T(8,128)}, u32[]{:S(2)}) copy-start(f32[3,256,256]{2,1,0:T(8,128)} %field.1) | copy-start | bytes 2359300
  24.4 93.2 %collective-permute-start.1 = (f32[3,128,256]{2,1,0:T(8,128)S(1)}, f32[3,128,256]{2,1,0:T(8,128)S(1)}, u32[]{:S(2)}, u32[]{:S(2)}) collective-permute-start(f32[3,128,256]{2,1,0:T(8,128)S(1)} %slice.7), channel_id=1, source_target_pairs={{32,0},{64,32},{96,64},{128,96},{160,128},{192,160},{224,192},{33,... | collective-permute-start | bytes 1179656 | tf_op jit(solution)/shard_map/ppermute | solution.py:24
  27.8 39.3 %copy-start.3 = (f32[1024]{0:T(1024)S(1)}, f32[1024]{0:T(1024)}, u32[]{:S(2)}) copy-start(f32[1024]{0:T(1024)} %param.7) | copy-start | bytes 12292
  64.1 3.8 %copy-start.1 = (f32[256,256]{1,0:T(8,128)}, f32[256,256]{1,0:T(8,128)S(1)}, u32[]{:S(2)}) copy-start(f32[256,256]{1,0:T(8,128)S(1)} %reshape.34.gram) | copy-start | bytes 786436
  117.6 0.7 copy-start.2

commit v2 on v0

v2 whole, which is shorter than its diff:
```python
import functools
import math

import jax
import jax.numpy as jnp
from jax import lax
from jax.experimental import pallas as pl
from jax.experimental.pallas import tpu as pltpu
from jax.sharding import PartitionSpec as P

SEC_NODES = 128
SPAN_XSEC_LEAF = ("span", "xsec", "leaf")
TILE = 8
LANES = 128
CHUNK = 256

highest = lax.Precision.HIGHEST
f32 = jnp.float32


class DeviceSum:
    def __init__(self, part, arrived, planes, gathered, sent, got):
        self.part, self.arrived, self.planes, self.gathered = part, arrived, planes, gathered
        self.sent, self.got = sent, got
        self.near, self.far = part.shape[0], planes.shape[0]
        self.leaves = lax.axis_size("leaf")
        self.chips = self.near // (2 * self.leaves)
        self.span, self.xsec, self.leaf = (lax.axis_index(name) for name in SPAN_XSEC_LEAF)
        self.own = self.xsec * self.leaves + self.leaf

    def place(self, step):
        chip = (self.xsec // 2 + (step // 2) % self.chips) % self.chips
        side = (self.leaf + step // (2 * self.chips)) % self.leaves
        return chip * 2 + (self.xsec + step % 2) % 2, side

    def in_slab(self, step):
        other, side = self.place(step)
        return {"xsec": other, "leaf": side}

    def slab_above(self, step):
        return {"span": (self.span + step) % self.far}

    def scatter(self, step):
        other, side = self.place(step)
        return pltpu.make_async_remote_copy(
            self.part.at[other * self.leaves + side], self.arrived.at[step],
            self.sent.at[0, step], self.got.at[0, step], self.in_slab(step),
        )

    def exchange(self, step):
        block = self.planes.at[self.span]
        return pltpu.make_async_remote_copy(
            block, block, self.sent.at[1, step], self.got.at[1, step], self.slab_above(step)
        )

    def gather(self, step):
        block = self.gathered.at[self.own]
        return pltpu.make_async_remote_copy(
            block, block, self.sent.at[2, step], self.got.at[2, step], self.in_slab(step)
        )

    def each(self, count, act):
        lax.fori_loop(1, count, lambda step, _: (act(step), 0)[1], 0)

    def greet(self):
        barrier = pltpu.get_barrier_semaphore()
        signal = lambda where: pl.semaphore_signal(barrier, inc=1, device_id=where)
        self.each(self.near, lambda step: signal(self.in_slab(step)))
        self.each(self.far, lambda step: signal(self.slab_above(step)))

    def meet(self):
        pl.semaphore_wait(pltpu.get_barrier_semaphore(), self.near + self.far - 2)

    def start_scatter(self):
        self.each(self.near, lambda step: self.scatter(step).start())

    def start_exchange(self):
        self.each(self.near, lambda step: self.scatter(step).wait_recv())
        block = self.part[self.own]
        for step in range(1, self.near):
            block = block + self.arrived[step]
        self.planes[self.span] = block
        self.each(self.far, lambda step: self.exchange(step).start())

    def start_gather(self):
        self.each(self.far, lambda step: self.exchange(step).wait_recv())
        block = self.planes[0]
        for other in range(1, self.far):
            block = block + self.planes[other]
        self.gathered[self.own] = block
        self.each(self.near, lambda step: self.gather(step).start())

    def finish(self, total):
        self.each(self.near, lambda step: self.gather(step).wait_recv())
        lines = self.part.shape[1]
        for other in range(self.near):
            total[lines * other : lines * (other + 1), :] = self.gathered[other]
        self.each(self.near, lambda step: self.scatter(step).wait_send())
        self.each(self.far, lambda step: self.exchange(step).wait_send())
        self.each(self.near, lambda step: self.gather(step).wait_send())

    def take(self, flat):
        lines = self.part.shape[1]
        for other in range(self.near):
            self.part[other] = flat[lines * other : lines * (other + 1), :]


def sum_scratch(near, far, lines):
    blocks = pltpu.VMEM((near, lines, LANES), f32)
    pairs = pltpu.SemaphoreType.DMA((3, near))
    return [blocks, blocks, pltpu.VMEM((far, lines, LANES), f32), blocks, pairs, pairs]


def dot_f32(a, b, over_a=1, over_b=0):
    return lax.dot_general(
        a, b, (((over_a,), (over_b,)), ((), ())), precision=highest, preferred_element_type=f32
    )


def dot_bf16(a, b):
    return jnp.dot(a, b, preferred_element_type=f32)


def in_three(x):
    high = x.astype(jnp.bfloat16)
    rest = x - high.astype(f32)
    middle = rest.astype(jnp.bfloat16)
    return high, middle, (rest - middle.astype(f32)).astype(jnp.bfloat16)


def over_lanes(column):
    return jnp.broadcast_to(column, (TILE, LANES))


def over_rows(row):
    return jnp.broadcast_to(row, (TILE, LANES))


def factor_block(block):
    count = LANES // TILE
    lane = lax.broadcasted_iota(jnp.int32, (TILE, LANES), 1)
    sub = lax.broadcasted_iota(jnp.int32, (TILE, LANES), 0)
    left = [block[TILE * i : TILE * i + TILE, :] for i in range(count)]
    right = [jnp.where(lane == sub + TILE * i, 1.0, 0.0).astype(f32) for i in range(count)]
    for k in range(count):
        own_left, own_right = left[k], right[k]
        at = TILE * k
        columns = [over_lanes(own_left[:, at + j : at + j + 1]) for j in range(TILE)]
        pivot_left, pivot_right, pivot_columns, inverse = [], [], [], []
        scale = jnp.zeros((TILE, LANES), f32)
        for j in range(TILE):
            pivot = over_rows(columns[j][j : j + 1, :])
            inverse.append(1.0 / pivot)
            pivot_left.append(over_rows(own_left[j : j + 1, :]))
            pivot_right.append(over_rows(own_right[j : j + 1, :]))
            pivot_columns.append([over_rows(columns[l][j : j + 1, :]) for l in range(TILE)])
            factor = jnp.where(sub > j, columns[j] * inverse[j], 0.0)
            for l in range(j + 1, TILE):
                columns[l] = columns[l] - factor * pivot_columns[j][l]
            own_left = own_left - factor * pivot_left[j]
            own_right = own_right - factor * pivot_right[j]
            scale = jnp.where(sub == j, lax.rsqrt(pivot), scale)
        for i in range(k + 1, count):
            columns = [over_lanes(left[i][:, at + j : at + j + 1]) for j in range(TILE)]
            row_left, row_right = left[i], right[i]
            for j in range(TILE):
                factor = columns[j] * inverse[j]
                for l in range(j + 1, TILE):
                    columns[l] = columns[l] - factor * pivot_columns[j][l]
                row_left = row_left - factor * pivot_left[j]
                row_right = row_right - factor * pivot_right[j]
            left[i], right[i] = row_left, row_right
        left[k] = jnp.where(lane >= sub + at, own_left * scale, 0.0)
        right[k] = own_right * scale
    return jnp.concatenate(left, 0), jnp.concatenate(right, 0)


def factor_into(gram_ref, upper_ref, inverse_ref):
    upper_a, lower_a = factor_block(gram_ref[:LANES, :])
    across = dot_f32(lower_a, gram_ref[LANES : 2 * LANES, :])
    corner = gram_ref[2 * LANES : 3 * LANES, :] - dot_f32(across, across, 0, 0)
    upper_b, lower_b = factor_block(corner)
    zero = jnp.zeros((LANES, LANES), f32)
    upper_ref[:LANES, :LANES] = upper_a
    upper_ref[:LANES, LANES:] = across
    upper_ref[LANES:, :LANES] = zero
    upper_ref[LANES:, LANES:] = upper_b
    inverse_a, inverse_b = lower_a.T, lower_b.T
    inverse_ref[:LANES, :LANES] = inverse_a
    inverse_ref[:LANES, LANES:] = -dot_f32(inverse_a, dot_f32(across, inverse_b))
    inverse_ref[LANES:, :LANES] = zero
    inverse_ref[LANES:, LANES:] = inverse_b


def put_product(flat, start, a, b):
    top = dot_f32(a[:, :LANES], b, 0, 0)
    flat[start : start + LANES, :] = top[:, :LANES]
    flat[start + LANES : start + 2 * LANES, :] = top[:, LANES:]
    flat[start + 2 * LANES : start + 3 * LANES, :] = dot_f32(a[:, LANES:], b[:, LANES:], 0, 0)


def from_blocks(flat, start):
    across = flat[start + LANES : start + 2 * LANES, :]
    top = jnp.concatenate([flat[start : start + LANES, :], across], 1)
    low = jnp.concatenate([across.T, flat[start + 2 * LANES : start + 3 * LANES, :]], 1)
    return jnp.concatenate([top, low], 0)


def gram_and_members(
    field, ends, direction, stiff, gram, elongation, forces,
    pick, spread, parts, below, table, flat, halo_sent, halo_got, *for_sum,
):
    total = DeviceSum(*for_sum)
    total.greet()
    components, own, width = field.shape
    nodes = own + below.shape[1]
    members = ends.shape[1]
    kept = jnp.where(total.span == 0, own, nodes)

    def halo(c):
        return pltpu.make_async_remote_copy(
            field.at[c, 2 * own - nodes : own], below.at[c], halo_sent.at[c], halo_got.at[c],
            total.slab_above(1),
        )

    flattened = field[...].reshape(components * own, width)
    put_product(flat, 0, flattened, flattened)
    total.take(flat)
    table[...] = jnp.concatenate(
        [direction[...], stiff[...], ends[...].astype(f32), jnp.zeros((2, members), f32)], 0
    ).T
    chunks = [slice(start, start + CHUNK) for start in range(0, members, CHUNK)]

    def split(c, start, ref):
        for p, piece in enumerate(in_three(ref[c])):
            parts[p, c, start : start + ref.shape[1], :] = piece

    def stretch(rows, cut):
        result = jnp.zeros((CHUNK, width), f32)
        for c in range(components):
            difference = dot_bf16(pick[rows, cut], parts[2, c, cut, :])
            difference = difference + dot_bf16(pick[rows, cut], parts[1, c, cut, :])
            difference = difference + dot_bf16(pick[rows, cut], parts[0, c, cut, :])
            result = result + table[rows, c : c + 1] * difference
        return result

    for c in range(components):
        split(c, 0, field)
    for rows in chunks:
        node = lax.broadcasted_iota(jnp.int32, (CHUNK, nodes), 1)
        node = jnp.where(node < kept, node, -1).astype(f32)
        chosen = jnp.where(node == table[rows, 4:5], 1.0, 0.0)
        chosen = chosen - jnp.where(node == table[rows, 5:6], 1.0, 0.0)
        pick[rows, :] = chosen.astype(jnp.bfloat16)
        node = lax.broadcasted_iota(jnp.int32, (nodes, CHUNK), 0)
        node = jnp.where(node < kept, node, -1)
        chosen = jnp.where(node == ends[0:1, rows], 1.0, 0.0)
        chosen = chosen - jnp.where(node == ends[1:2, rows], 1.0, 0.0)
        spread[:, rows] = chosen.astype(jnp.bfloat16)
        elongation[rows, :] = stretch(rows, slice(0, own))
    total.meet()
    total.start_scatter()
    for c in range(components - 1):
        halo(c).start()
    total.start_exchange()
    halo(components - 1).start()
    for c in range(components):
        halo(c).wait_recv()
        split(c, own, below)
    total.start_gather()
    forces[...] = jnp.zeros_like(forces)
    for rows in chunks:
        whole = elongation[rows, :] + stretch(rows, slice(own, nodes))
        elongation[rows, :] = whole
        pull = whole * table[rows, 3:4]
        for c in range(components):
            high, middle, low = in_three(table[rows, c : c + 1] * pull)
            push = dot_bf16(spread[:, rows], low) + dot_bf16(spread[:, rows], middle)
            forces[c] = forces[c] + (push + dot_bf16(spread[:, rows], high))
    total.finish(gram)
    for c in range(components):
        halo(c).wait_send()


def first_stage(field, ends, direction, stiff):
    components, own, width = field.shape
    nodes, members = own + SEC_NODES, ends.shape[1]
    near, far = lax.axis_size("xsec") * lax.axis_size("leaf"), lax.axis_size("span")
    halo = pltpu.SemaphoreType.DMA((components,))
    return pl.pallas_call(
        gram_and_members,
        out_shape=(
            jax.ShapeDtypeStruct((3 * LANES, LANES), f32),
            jax.ShapeDtypeStruct((members, width), f32),
            jax.ShapeDtypeStruct((components, nodes, width), f32),
        ),
        scratch_shapes=[
            pltpu.VMEM((members, nodes), jnp.bfloat16),
            pltpu.VMEM((nodes, members), jnp.bfloat16),
            pltpu.VMEM((3, components, nodes, width), jnp.bfloat16),
            pltpu.VMEM((components, SEC_NODES, width), f32),
            pltpu.VMEM((members, TILE), f32),
            pltpu.VMEM((3 * LANES, LANES), f32),
            halo,
            halo,
            *sum_scratch(near, far, 3 * LANES // near),
        ],
        compiler_params=pltpu.CompilerParams(
            collective_id=0, has_side_effects=True, vmem_limit_bytes=60 << 20
        ),
        name="gram_and_members",
    )(field, ends, direction, stiff.reshape(1, -1))


def factor_and_sums(
    gram, field, elongation, stiff, raw, upper, inverse, first, sums, returned,
    landed, flat, halo_sent, halo_got, *for_sum,
):
    total = DeviceSum(*for_sum)
    total.greet()
    components, count, width = landed.shape
    own = raw.shape[1] - count

    def halo(c):
        return pltpu.make_async_remote_copy(
            raw.at[c, own : own + count], landed.at[c], halo_sent.at[c], halo_got.at[c],
            total.slab_above(total.far - 1),
        )

    factor_into(gram, upper, inverse)
    total.meet()
    for c in range(components):
        halo(c).start()
    transform = inverse[...]
    flattened = field[...].reshape(first.shape)
    first[...] = dot_f32(flattened, transform)
    put_product(flat, 0, first[...], first[...])
    stretch = dot_f32(elongation[...], transform)
    pull = stretch * jnp.broadcast_to(stiff[...], (TILE, stiff.shape[1])).T[:, :1]
    put_product(flat, 3 * LANES, stretch, pull)
    total.take(flat)
    total.start_scatter()
    total.start_exchange()
    for c in range(components):
        halo(c).wait_recv()
    returned[...] = landed[...]
    total.start_gather()
    total.finish(sums)
    for c in range(components):
        halo(c).wait_send()


def second_stage(gram, field, elongation, stiff, raw):
    components, own, width = field.shape
    square = jax.ShapeDtypeStruct((width, width), f32)
    near, far = lax.axis_size("xsec") * lax.axis_size("leaf"), lax.axis_size("span")
    halo = pltpu.SemaphoreType.DMA((components,))
    return pl.pallas_call(
        factor_and_sums,
        out_shape=(
            square,
            square,
            jax.ShapeDtypeStruct((components * own, width), f32),
            jax.ShapeDtypeStruct((6 * LANES, LANES), f32),
            jax.ShapeDtypeStruct((components, SEC_NODES, width), f32),
        ),
        scratch_shapes=[
            pltpu.VMEM((components, SEC_NODES, width), f32),
            pltpu.VMEM((6 * LANES, LANES), f32),
            halo,
            halo,
            *sum_scratch(near, far, 6 * LANES // near),
        ],
        compiler_params=pltpu.CompilerParams(
            collective_id=1, has_side_effects=True, vmem_limit_bytes=60 << 20
        ),
        name="factor_and_sums",
    )(gram, field, elongation, stiff.reshape(1, -1), raw)


def outputs_kernel(
    total_rows, gram, sums, upper_first, inverse_first, first, raw, returned,
    basis, forces, reduced, coef, energy, upper, inverse,
):
    components, own, width = forces.shape
    root = math.sqrt(total_rows)
    low = own - returned.shape[1]
    factor_into(sums, upper, inverse)
    transform = inverse[...]
    basis[...] = dot_f32(first[...], transform) * root
    both = dot_f32(inverse_first[...], transform) * root
    for c in range(components):
        forces[c, :low, :] = dot_f32(raw[c, :low, :], both)
        forces[c, low:, :] = dot_f32(raw[c, low:own, :] + returned[c], both)
    product = from_blocks(sums, 3 * LANES)
    reduced[...] = dot_f32(transform, dot_f32(product, transform), 0, 0)
    coef[...] = dot_f32(upper[...], upper_first[...]) * (1.0 / root)
    diagonal = lax.broadcasted_iota(jnp.int32, (LANES, LANES), 0)
    diagonal = diagonal == lax.broadcasted_iota(jnp.int32, (LANES, LANES), 1)
    for half, start in enumerate((0, 2 * LANES)):
        squares = jnp.sum(jnp.where(diagonal, gram[start : start + LANES, :], 0.0), 0, keepdims=True)
        energy[:, half * LANES : (half + 1) * LANES] = jnp.log(squares / total_rows)


def outputs(gram, sums, upper, inverse, first, raw, returned, total_rows):
    components, _, width = raw.shape
    own = first.shape[0] // components
    square = jax.ShapeDtypeStruct((width, width), f32)
    return pl.pallas_call(
        functools.partial(outputs_kernel, total_rows),
        out_shape=(
            jax.ShapeDtypeStruct(first.shape, f32),
            jax.ShapeDtypeStruct((components, own, width), f32),
            square,
            square,
            jax.ShapeDtypeStruct((1, width), f32),
        ),
        scratch_shapes=[pltpu.VMEM((width, width), f32)] * 2,
        compiler_params=pltpu.CompilerParams(vmem_limit_bytes=60 << 20),
        name="outputs",
    )(gram, sums, upper, inverse, first, raw, returned)


def local(snapshots, member_ends, member_dir, member_stiff):
    components, node_count, width = snapshots.shape
    devices_all = lax.axis_size(SPAN_XSEC_LEAF)
    total_rows = components * node_count * devices_all
    gram, elongation, raw = first_stage(snapshots, member_ends, member_dir, member_stiff)
    upper, inverse, first, sums, returned = second_stage(
        gram, snapshots, elongation, member_stiff, raw
    )
    basis, forces, reduced, coef, energy = outputs(
        gram, sums, upper, inverse, first, raw, returned, total_rows
    )
    return (basis.reshape(snapshots.shape), forces, reduced, coef, energy.reshape(width))


def solution(mesh):
    return jax.shard_map(
        local,
        mesh=mesh,
        in_specs=(
            P(None, SPAN_XSEC_LEAF, None),
            P(None, SPAN_XSEC_LEAF),
            P(None, SPAN_XSEC_LEAF),
            P(SPAN_XSEC_LEAF),
        ),
        out_specs=(P(None, SPAN_XSEC_LEAF, None), P(None, SPAN_XSEC_LEAF, None), P(), P(), P()),
        check_vma=False,
    )
```

time: 159 us -> 89.2 us (0.56)
  blocking collectives: 79.7 us -> 0 us
  Pallas kernels: 39.4 us -> 88.4 us
  starting transfers between devices: 17.9 us -> 0 us
  local copies, waits for them, and re-layouts: 12.5 us -> 0 us
  waiting for transfers between devices: 6.74 us -> 0 us
    all_to_all x6 -> x0, blocking collectives: 79.7 us -> none  [the longest x2 30.6 us: sum_in_two_steps(): lax.all_to_all(nearer, far, split_axis=0, concat_axis=0, tiled=True)]
    pallas_call x3, Pallas kernels: 39.4 us -> 88.4 us  [the longest x1 39.3 us: second_stage(): pl.pallas_call(factor_and_sums, out_shape=(square, square, jax.ShapeDtype...]
    all_to_all x2 -> x0, starting transfers between devices: 12.2 us -> none  [from_everyone(): lax.all_to_all(jnp.broadcast_to(array[None], (length, *array.shape)), axi...]
    ppermute x2 -> x0, starting transfers between devices: 5.68 us -> none  [shifted(): return lax.ppermute(array, axis, pairs)]
    all_to_all x2 -> x0, waiting for transfers between devices: 4.09 us -> none  [from_everyone(): lax.all_to_all(jnp.broadcast_to(array[None], (length, *array.shape)), axi...]
    ppermute x2 -> x0, waiting for transfers between devices: 2.65 us -> none  [shifted(): return lax.ppermute(array, axis, pairs)]
    gather x1 -> x0, local copies, waits for them, and re-layouts: 2.34 us -> none  [local(): column_energy = jnp.log(jnp.diagonal(gram) / total_rows)]
    broadcast_in_dim x5 -> x0, local copies, waits for them, and re-layouts: 2.32 us -> none  [the longest x4 1.7 us: from_everyone(): jnp.broadcast_to(array[None], (length, *array.shape))]
  transfers between devices with their start and end apart: 4 -> 0, of which waited for: 2 -> 0; matrix products, arithmetic and copies ran while one was open for 5% -> 0% of each run, Pallas kernels for 5% -> 0%
where the time goes in v2:
time: 89.2 us; the launch traced here: 89 us
  Pallas kernels  88.4 us (99%)
    pallas_call x1, Pallas kernels, second_stage(): pl.pallas_call(factor_and_sums, out_shape=(square, square, jax.ShapeDtype...  39.3 us
    pallas_call x1, Pallas kernels, first_stage(): pl.pallas_call(gram_and_members, out_shape=(jax.ShapeDtypeStruct((3 * LAN...  34.7 us
    pallas_call x1, Pallas kernels, outputs(): pl.pallas_call(functools.partial(outputs_kernel, total_rows), out_shape=(...  14.4 us

profile of v2, /device:TPU:1, one launch (start us, length us, event | category | flops | bytes accessed | tf_op | source)
XLA Modules:
  0.0 89.0 jit_solution(13065924558401892614)
XLA Ops:
  0.6 34.7 %gram_and_members.1 = (f32[384,128]{1,0:T(8,128)}, f32[1024,256]{1,0:T(8,128)}, f32[3,384,256]{2,1,0:T(8,128)}) custom-call(f32[3,256,256]{2,1,0:T(8,128)} %field.3, s32[2,1024]{1,0:T(2,128)} %ends.1, f32[3,1024]{1,0:T(4,128)} %direction.1, f32[1,1024]{1,0:T(1,128)} %bitcast.3), custom_call_target="tpu_custom_call" | custom-call | tf_op jit(solution)/shard_map/gram_and_members/pallas_call | solution.py:290
  35.3 39.3 %factor_and_sums.1 = (f32[256,256]{1,0:T(8,128)}, f32[256,256]{1,0:T(8,128)}, f32[768,256]{1,0:T(8,128)}, f32[768,128]{1,0:T(8,128)}, f32[3,128,256]{2,1,0:T(8,128)}) custom-call(f32[384,128]{1,0:T(8,128)} %get-tuple-element.18.gram, f32[3,256,256]{2,1,0:T(8,128)} %field.3, f32[1024,256]{1,0:T(8,128)} %get-tuple-element.19.elongation, f32[1,1024]{1,0:T(1,128)} %bitcast.4, ...), custom_call_target="tpu_custom_call" | custom-call | tf_op jit(solution)/shard_map/factor_and_sums/pallas_call | solution.py:358
  74.6 14.4 %outputs.1 = (f32[768,256]{1,0:T(8,128)}, f32[3,256,256]{2,1,0:T(8,128)}, f32[256,256]{1,0:T(8,128)}, f32[256,256]{1,0:T(8,128)}, f32[1,256]{1,0:T(1,128)}) custom-call(f32[384,128]{1,0:T(8,128)} %get-tuple-element.18.gram, f32[768,128]{1,0:T(8,128)} %get-tuple-element.21.sums, f32[256,256]{1,0:T(8,128)} %get-tuple-element.22.upper_first, ...), custom_call_target="tpu_custom_call" | custom-call | tf_op jit(solution)/shard_map/outputs/pallas_call | solution.py:409

commit v3 on v2

--- a/solution.py
+++ b/solution.py
@@ -27,18 +27,25 @@
         self.chips = self.near // (2 * self.leaves)
         self.span, self.xsec, self.leaf = (lax.axis_index(name) for name in SPAN_XSEC_LEAF)
         self.own = self.xsec * self.leaves + self.leaf
+        self.chip, self.core = lax.div(self.xsec, 2), lax.rem(self.xsec, 2)
+        around = lambda steps, length: min(steps, length - steps)
+        hops = lambda step: around(step // 2 % self.chips, self.chips) + around(
+            step // (2 * self.chips), self.leaves
+        )
+        self.slab_steps = sorted(range(1, self.near), key=lambda step: -hops(step))
+        self.span_steps = sorted(range(1, self.far), key=lambda step: -around(step, self.far))
 
     def place(self, step):
-        chip = (self.xsec // 2 + (step // 2) % self.chips) % self.chips
-        side = (self.leaf + step // (2 * self.chips)) % self.leaves
-        return chip * 2 + (self.xsec + step % 2) % 2, side
+        chip = lax.rem(self.chip + step // 2 % self.chips, self.chips)
+        core = lax.rem(self.core + step % 2, 2)
+        return chip * 2 + core, lax.rem(self.leaf + step // (2 * self.chips), self.leaves)
 
     def in_slab(self, step):
         other, side = self.place(step)
         return {"xsec": other, "leaf": side}
 
     def slab_above(self, step):
-        return {"span": (self.span + step) % self.far}
+        return {"span": lax.rem(self.span + step, self.far)}
 
     def scatter(self, step):
         other, side = self.place(step)
@@ -60,7 +67,8 @@
         )
 
     def each(self, count, act):
-        lax.fori_loop(1, count, lambda step, _: (act(step), 0)[1], 0)
+        for step in self.slab_steps if count == self.near else self.span_steps:
+            act(step)
 
     def greet(self):
         barrier = pltpu.get_barrier_semaphore()
@@ -115,6 +123,18 @@
     return lax.dot_general(
         a, b, (((over_a,), (over_b,)), ((), ())), precision=highest, preferred_element_type=f32
     )
+
+
+def in_two(x):
+    high = x.astype(jnp.bfloat16)
+    return high, (x - high.astype(f32)).astype(jnp.bfloat16)
+
+
+def dot_split(a, b, over_a=1, over_b=0):
+    (high_a, low_a), (high_b, low_b) = in_two(a), in_two(b)
+    dims = (((over_a,), (over_b,)), ((), ()))
+    one = lambda x, y: lax.dot_general(x, y, dims, preferred_element_type=f32)
+    return one(high_a, low_b) + one(low_a, high_b) + one(high_a, high_b)
 
 
 def dot_bf16(a, b):
@@ -192,11 +212,11 @@
     inverse_ref[LANES:, LANES:] = inverse_b
 
 
-def put_product(flat, start, a, b):
-    top = dot_f32(a[:, :LANES], b, 0, 0)
+def put_product(flat, start, a, b, dot):
+    top = dot(a[:, :LANES], b, 0, 0)
     flat[start : start + LANES, :] = top[:, :LANES]
     flat[start + LANES : start + 2 * LANES, :] = top[:, LANES:]
-    flat[start + 2 * LANES : start + 3 * LANES, :] = dot_f32(a[:, LANES:], b[:, LANES:], 0, 0)
+    flat[start + 2 * LANES : start + 3 * LANES, :] = dot(a[:, LANES:], b[:, LANES:], 0, 0)
 
 
 def from_blocks(flat, start):
@@ -207,8 +227,8 @@
 
 
 def gram_and_members(
-    field, ends, direction, stiff, gram, elongation, forces,
-    pick, spread, parts, below, table, flat, halo_sent, halo_got, *for_sum,
+    field, ends, direction, stiff, gram, elongation_out, forces_out,
+    elongation, forces, out_done, pick, spread, parts, below, table, flat, halo_sent, halo_got, *for_sum,
 ):
     total = DeviceSum(*for_sum)
     total.greet()
@@ -224,7 +244,7 @@
         )
 
     flattened = field[...].reshape(components * own, width)
-    put_product(flat, 0, flattened, flattened)
+    put_product(flat, 0, flattened, flattened, dot_f32)
     total.take(flat)
     table[...] = jnp.concatenate(
         [direction[...], stiff[...], ends[...].astype(f32), jnp.zeros((2, members), f32)], 0
@@ -235,9 +255,8 @@
         for p, piece in enumerate(in_three(ref[c])):
             parts[p, c, start : start + ref.shape[1], :] = piece
 
-    def stretch(rows, cut):
-        result = jnp.zeros((CHUNK, width), f32)
-        for c in range(components):
+    def stretch(rows, cut, which, result):
+        for c in which:
             difference = dot_bf16(pick[rows, cut], parts[2, c, cut, :])
             difference = difference + dot_bf16(pick[rows, cut], parts[1, c, cut, :])
             difference = difference + dot_bf16(pick[rows, cut], parts[0, c, cut, :])
@@ -257,29 +276,45 @@
         chosen = jnp.where(node == ends[0:1, rows], 1.0, 0.0)
         chosen = chosen - jnp.where(node == ends[1:2, rows], 1.0, 0.0)
         spread[:, rows] = chosen.astype(jnp.bfloat16)
-        elongation[rows, :] = stretch(rows, slice(0, own))
     total.meet()
     total.start_scatter()
     for c in range(components - 1):
         halo(c).start()
+    for rows in chunks:
+        zero = jnp.zeros((CHUNK, width), f32)
+        elongation[rows, :] = stretch(rows, slice(0, own), range(components), zero)
     total.start_exchange()
     halo(components - 1).start()
-    for c in range(components):
+    for c in range(components - 1):
         halo(c).wait_recv()
         split(c, own, below)
+    for rows in chunks:
+        elongation[rows, :] = stretch(
+            rows, slice(own, nodes), range(components - 1), elongation[rows, :]
+        )
     total.start_gather()
+    halo(components - 1).wait_recv()
+    split(components - 1, own, below)
     forces[...] = jnp.zeros_like(forces)
     for rows in chunks:
-        whole = elongation[rows, :] + stretch(rows, slice(own, nodes))
+        whole = stretch(rows, slice(own, nodes), [components - 1], elongation[rows, :])
         elongation[rows, :] = whole
         pull = whole * table[rows, 3:4]
         for c in range(components):
             high, middle, low = in_three(table[rows, c : c + 1] * pull)
             push = dot_bf16(spread[:, rows], low) + dot_bf16(spread[:, rows], middle)
             forces[c] = forces[c] + (push + dot_bf16(spread[:, rows], high))
+    leave = [
+        pltpu.make_async_copy(elongation, elongation_out, out_done.at[0]),
+        pltpu.make_async_copy(forces, forces_out, out_done.at[1]),
+    ]
+    for copy in leave:
+        copy.start()
     total.finish(gram)
     for c in range(components):
         halo(c).wait_send()
+    for copy in leave:
+        copy.wait()
 
 
 def first_stage(field, ends, direction, stiff):
@@ -294,7 +329,15 @@
             jax.ShapeDtypeStruct((members, width), f32),
             jax.ShapeDtypeStruct((components, nodes, width), f32),
         ),
+        out_specs=(
+            pl.BlockSpec(memory_space=pltpu.VMEM),
+            pl.BlockSpec(memory_space=pl.ANY),
+            pl.BlockSpec(memory_space=pl.ANY),
+        ),
         scratch_shapes=[
+            pltpu.VMEM((members, width), f32),
+            pltpu.VMEM((components, nodes, width), f32),
+            pltpu.SemaphoreType.DMA((2,)),
             pltpu.VMEM((members, nodes), jnp.bfloat16),
             pltpu.VMEM((nodes, members), jnp.bfloat16),
             pltpu.VMEM((3, components, nodes, width), jnp.bfloat16),
@@ -313,8 +356,8 @@
 
 
 def factor_and_sums(
-    gram, field, elongation, stiff, raw, upper, inverse, first, sums, returned,
-    landed, flat, halo_sent, halo_got, *for_sum,
+    gram, field_in, elongation_in, stiff, raw_in, upper, first, forces, sums,
+    inverse, field, elongation, raw, in_done, landed, flat, halo_sent, halo_got, *for_sum,
 ):
     total = DeviceSum(*for_sum)
     total.greet()
@@ -327,23 +370,35 @@
             total.slab_above(total.far - 1),
         )
 
+    enter = [
+        pltpu.make_async_copy(source, target, in_done.at[i])
+        for i, (source, target) in enumerate(
+            ((raw_in, raw), (field_in, field), (elongation_in, elongation))
+        )
+    ]
+    for copy in enter:
+        copy.start()
     factor_into(gram, upper, inverse)
+    for copy in enter:
+        copy.wait()
     total.meet()
     for c in range(components):
         halo(c).start()
     transform = inverse[...]
     flattened = field[...].reshape(first.shape)
     first[...] = dot_f32(flattened, transform)
-    put_product(flat, 0, first[...], first[...])
+    put_product(flat, 0, first[...], first[...], dot_split)
     stretch = dot_f32(elongation[...], transform)
     pull = stretch * jnp.broadcast_to(stiff[...], (TILE, stiff.shape[1])).T[:, :1]
-    put_product(flat, 3 * LANES, stretch, pull)
+    put_product(flat, 3 * LANES, stretch, pull, dot_split)
     total.take(flat)
     total.start_scatter()
     total.start_exchange()
     for c in range(components):
         halo(c).wait_recv()
-    returned[...] = landed[...]
+        forces[c, : own - count, :] = dot_f32(raw[c, : own - count, :], transform)
+        top = raw[c, own - count : own, :] + landed[c]
+        forces[c, own - count :, :] = dot_f32(top, transform)
     total.start_gather()
     total.finish(sums)
     for c in range(components):
@@ -359,12 +414,20 @@
         factor_and_sums,
         out_shape=(
             square,
-            square,
             jax.ShapeDtypeStruct((components * own, width), f32),
+            jax.ShapeDtypeStruct((components, own, width), f32),
             jax.ShapeDtypeStruct((6 * LANES, LANES), f32),
-            jax.ShapeDtypeStruct((components, SEC_NODES, width), f32),
-        ),
+        ),
+        in_specs=[
+            pl.BlockSpec(memory_space=space)
+            for space in (pltpu.VMEM, pl.ANY, pl.ANY, pltpu.VMEM, pl.ANY)
+        ],
         scratch_shapes=[
+            pltpu.VMEM((width, width), f32),
+            pltpu.VMEM(field.shape, f32),
+            pltpu.VMEM(elongation.shape, f32),
+            pltpu.VMEM(raw.shape, f32),
+            pltpu.SemaphoreType.DMA((3,)),
             pltpu.VMEM((components, SEC_NODES, width), f32),
             pltpu.VMEM((6 * LANES, LANES), f32),
             halo,
@@ -378,23 +441,49 @@
     )(gram, field, elongation, stiff.reshape(1, -1), raw)
 
 
+def refine(gap, rounds):
+    row = lax.broadcasted_iota(jnp.int32, gap.shape, 0)
+    column = lax.broadcasted_iota(jnp.int32, gap.shape, 1)
+    share = jnp.where(row < column, 1.0, jnp.where(row == column, 0.5, 0.0))
+    change = None
+    for last in [False] * (rounds - 1) + [True]:
+        half = gap * share
+        change = -half if change is None else change - half - dot_split(change, half)
+        if not last:
+            image = dot_split(gap, half)
+            gap = dot_split(half, half + image, 0, 0) - (image + image.T)
+    return change, gap
+
+
 def outputs_kernel(
-    total_rows, gram, sums, upper_first, inverse_first, first, raw, returned,
-    basis, forces, reduced, coef, energy, upper, inverse,
+    total_rows, gram, sums, upper_first, first, forces_first,
+    basis, forces, reduced, coef, energy, upper, inverse, change, growth,
 ):
     components, own, width = forces.shape
     root = math.sqrt(total_rows)
-    low = own - returned.shape[1]
-    factor_into(sums, upper, inverse)
-    transform = inverse[...]
-    basis[...] = dot_f32(first[...], transform) * root
-    both = dot_f32(inverse_first[...], transform) * root
+    row = lax.broadcasted_iota(jnp.int32, (width, width), 0)
+    column = lax.broadcasted_iota(jnp.int32, (width, width), 1)
+    identity = jnp.where(row == column, 1.0, 0.0)
+    start = from_blocks(sums, 0) - identity
+    step, gap = refine(start, 2)
+    change[...] = step
+    whole = start + step.T + dot_split(step, start, 0, 0)
+    growth[...] = jnp.where(row <= column, whole, 0.0)
+
+    @pl.when(jnp.logical_not(jnp.sum(gap * gap) < 1e-4))
+    def _():
+        factor_into(sums, upper, inverse)
+        change[...] = inverse[...] - identity
+        growth[...] = upper[...] - identity
+
+    step = change[...]
+    basis[...] = (first[...] + dot_split(first[...], step)) * root
     for c in range(components):
-        forces[c, :low, :] = dot_f32(raw[c, :low, :], both)
-        forces[c, low:, :] = dot_f32(raw[c, low:own, :] + returned[c], both)
+        forces[c] = (forces_first[c] + dot_split(forces_first[c], step)) * root
     product = from_blocks(sums, 3 * LANES)
-    reduced[...] = dot_f32(transform, dot_f32(product, transform), 0, 0)
-    coef[...] = dot_f32(upper[...], upper_first[...]) * (1.0 / root)
+    product = product + dot_split(product, step)
+    reduced[...] = product + dot_split(step, product, 0, 0)
+    coef[...] = (upper_first[...] + dot_split(growth[...], upper_first[...])) * (1.0 / root)
     diagonal = lax.broadcasted_iota(jnp.int32, (LANES, LANES), 0)
     diagonal = diagonal == lax.broadcasted_iota(jnp.int32, (LANES, LANES), 1)
     for half, start in enumerate((0, 2 * LANES)):
@@ -402,36 +491,30 @@
         energy[:, half * LANES : (half + 1) * LANES] = jnp.log(squares / total_rows)
 
 
-def outputs(gram, sums, upper, inverse, first, raw, returned, total_rows):
-    components, _, width = raw.shape
-    own = first.shape[0] // components
+def outputs(gram, sums, upper, first, forces, total_rows):
+    width = forces.shape[2]
     square = jax.ShapeDtypeStruct((width, width), f32)
     return pl.pallas_call(
         functools.partial(outputs_kernel, total_rows),
         out_shape=(
             jax.ShapeDtypeStruct(first.shape, f32),
-            jax.ShapeDtypeStruct((components, own, width), f32),
+            jax.ShapeDtypeStruct(forces.shape, f32),
             square,
             square,
             jax.ShapeDtypeStruct((1, width), f32),
         ),
-        scratch_shapes=[pltpu.VMEM((width, width), f32)] * 2,
+        scratch_shapes=[pltpu.VMEM((width, width), f32)] * 4,
         compiler_params=pltpu.CompilerParams(vmem_limit_bytes=60 << 20),
         name="outputs",
-    )(gram, sums, upper, inverse, first, raw, returned)
+    )(gram, sums, upper, first, forces)
 
 
 def local(snapshots, member_ends, member_dir, member_stiff):
     components, node_count, width = snapshots.shape
-    devices_all = lax.axis_size(SPAN_XSEC_LEAF)
-    total_rows = components * node_count * devices_all
+    total_rows = components * node_count * lax.axis_size(SPAN_XSEC_LEAF)
     gram, elongation, raw = first_stage(snapshots, member_ends, member_dir, member_stiff)
-    upper, inverse, first, sums, returned = second_stage(
-        gram, snapshots, elongation, member_stiff, raw
-    )
-    basis, forces, reduced, coef, energy = outputs(
-        gram, sums, upper, inverse, first, raw, returned, total_rows
-    )
+    upper, first, forces, sums = second_stage(gram, snapshots, elongation, member_stiff, raw)
+    basis, forces, reduced, coef, energy = outputs(gram, sums, upper, first, forces, total_rows)
     return (basis.reshape(snapshots.shape), forces, reduced, coef, energy.reshape(width))
 
 

time: 89.2 us -> 74.1 us (0.83)
  Pallas kernels: 88.4 us -> 73.3 us
    pallas_call x1, Pallas kernels: 14.4 us -> 5.31 us  [outputs(): pl.pallas_call(functools.partial(outputs_kernel, total_rows), out_shape=(...]
    pallas_call x1, Pallas kernels: 34.7 us -> 31 us  [first_stage(): pl.pallas_call(gram_and_members, out_shape=(jax.ShapeDtypeStruct((3 * LAN...]
    pallas_call x1, Pallas kernels: 39.3 us -> 37 us  [second_stage(): pl.pallas_call(factor_and_sums, out_shape=(square, jax.ShapeDtypeStruct((...]
where the time goes in v3:
time: 74.1 us; the launch traced here: 73.9 us
  Pallas kernels  73.3 us (99%)
    pallas_call x1, Pallas kernels, second_stage(): pl.pallas_call(factor_and_sums, out_shape=(square, jax.ShapeDtypeStruct((...  37 us
    pallas_call x1, Pallas kernels, first_stage(): pl.pallas_call(gram_and_members, out_shape=(jax.ShapeDtypeStruct((3 * LAN...  31 us
    pallas_call x1, Pallas kernels, outputs(): pl.pallas_call(functools.partial(outputs_kernel, total_rows), out_shape=(...  5.31 us

profile of v3, /device:TPU:1, one launch (start us, length us, event | category | flops | bytes accessed | tf_op | source)
XLA Modules:
  0.0 73.9 jit_solution(5232411053214872191)
XLA Ops:
  0.6 31.0 %gram_and_members.1 = (f32[384,128]{1,0:T(8,128)}, f32[1024,256]{1,0:T(8,128)}, f32[3,384,256]{2,1,0:T(8,128)}) custom-call(f32[3,256,256]{2,1,0:T(8,128)} %field_in.1, s32[2,1024]{1,0:T(2,128)} %ends.1, f32[3,1024]{1,0:T(4,128)} %direction.1, f32[1,1024]{1,0:T(1,128)} %bitcast.3), custom_call_target="tpu_custom_call" | custom-call | tf_op jit(solution)/shard_map/gram_and_members/pallas_call | solution.py:325
  31.6 37.0 %factor_and_sums.1 = (f32[256,256]{1,0:T(8,128)}, f32[768,256]{1,0:T(8,128)}, f32[3,256,256]{2,1,0:T(8,128)}, f32[768,128]{1,0:T(8,128)}) custom-call(f32[384,128]{1,0:T(8,128)} %get-tuple-element.17.gram, f32[3,256,256]{2,1,0:T(8,128)} %field_in.1, f32[1024,256]{1,0:T(8,128)} %get-tuple-element.18.elongation_in, f32[1,1024]{1,0:T(1,128)} %bitcast.4, ...), custom_call_target="tpu_custom_call" | custom-call | tf_op jit(solution)/shard_map/factor_and_sums/pallas_call | solution.py:413
  68.6 5.3 %outputs.1 = (f32[768,256]{1,0:T(8,128)}, f32[3,256,256]{2,1,0:T(8,128)}, f32[256,256]{1,0:T(8,128)}, f32[256,256]{1,0:T(8,128)}, f32[1,256]{1,0:T(1,128)}) custom-call(f32[384,128]{1,0:T(8,128)} %get-tuple-element.17.gram, f32[768,128]{1,0:T(8,128)} %get-tuple-element.20.sums, f32[256,256]{1,0:T(8,128)} %get-tuple-element.21.upper_first, ...), custom_call_target="tpu_custom_call" | custom-call | tf_op jit(solution)/shard_map/outputs/pallas_call | solution.py:497
